TPU v7x, 32 devices: a whole 2x2x4 slice. The times are simulated.
32 devices in a mesh: batch: 4 (over x, core), vocab: 8 (over z, y).
Axes of the slice: x: 2, y: 2, z: 4, core: 2. Of those that a mesh axis runs over, the one named last changes fastest.
Arguments:
- logits: float32 [256, 152064], P('batch', 'vocab'), may hold values from -18 to 350
- history: int32 [256, 4096], P('batch', 'vocab'), may hold values from 0 to 152063, as said below
- history_weight: bfloat16 [256, 4096], P('batch', 'vocab'), may hold values from 0.25 to 2
- lengths: int32 [256], P('batch'), may hold values from 1 to 4096
- repetition: float32 [256], P('batch'), may hold values from 1.1 to 2
- frequency: float32 [256], P('batch'), may hold values from 0.05 to 0.5
- presence: float32 [256], P('batch'), may hold values from 0.1 to 1.5
Outputs:
- log_probs: float32 [256, 152064], P('batch', 'vocab')
Inputs may be any that keep to these rules, and one draw needn't show every extreme that they name: `history`: split each sequence's positions into 8 aligned blocks of equal length and the vocabulary into 8 equal ranges: within one block at most 128 ids fall in any one range.
All inputs are finite; a program needn't handle non-finite values.
Results may differ from a plain program's by a relative error of at most 0.0003.
Values may be sent and summed in bfloat16 or wider, within the bound.
No kernel may reach another device: no remote copies, remote signals or barrier semaphores. Data moves between devices by JAX's collectives and lax.ppermute only.
A program may use at most 64 MiB of HBM per device.

v0:
```python
import jax
import jax.numpy as jnp
from jax import lax
from jax.sharding import PartitionSpec as P


def tally(token_ids, token_weight, lengths, first, column0, width):
    seqs, span = token_ids.shape
    blocks = -(-width // 128)
    stride = 1
    for divisor in range(1, min(span, 1024) + 1):
        if span % divisor == 0:
            stride = divisor
    group_size = 4

    def one_group(packed):
        group_ids, group_weight, group_length = packed
        total = jnp.zeros((group_size, blocks, 256), jnp.float32)
        for block_index in range(span // stride):
            lower = block_index * stride
            piece_ids = group_ids[:, lower : lower + stride]
            piece_weight = group_weight[:, lower : lower + stride]
            positions = first + lower + jnp.arange(stride, dtype=jnp.int32)
            local = piece_ids - column0
            inside = (local >= 0) & (local < width) & (positions[None, :] < group_length[:, None])
            upper_index = jnp.where(inside, local // 128, -1)
            lower_index = jnp.where(inside, local % 128, -1)
            hot_upper = (upper_index[:, :, None] == jnp.arange(blocks, dtype=jnp.int32)).astype(
                jnp.bfloat16
            )
            hot_lower = (lower_index[:, :, None] == jnp.arange(128, dtype=jnp.int32)).astype(
                jnp.bfloat16
            )
            paired = jnp.concatenate([hot_lower, hot_lower * piece_weight[:, :, None]], axis=2)
            total = total + jnp.einsum(
                "sph,spl->shl", hot_upper, paired, preferred_element_type=jnp.float32
            )
        return total

    result = lax.map(
        one_group,
        (
            token_ids.reshape(seqs // group_size, group_size, span),
            token_weight.reshape(seqs // group_size, group_size, span),
            lengths.reshape(seqs // group_size, group_size),
        ),
    )
    result = result.reshape(seqs, blocks, 256)
    counts = result[:, :, :128].reshape(seqs, blocks * 128)[:, :width]
    weighted = result[:, :, 128:].reshape(seqs, blocks * 128)[:, :width]
    return (counts, weighted)


def body(logits, history, history_weight, lengths, repetition, frequency, presence):
    width = logits.shape[1]
    seqs, span = history.shape
    shards = lax.axis_size("vocab")
    slots = max(2, 2 * span // shards)
    positions = lax.axis_index("vocab") * span + jnp.arange(span, dtype=jnp.int32)
    valid = positions[None, :] < lengths[:, None]
    owner = jnp.where(valid, history // width, shards)
    order_index = jnp.arange(span, dtype=jnp.int32)
    earlier = order_index[None, :] < order_index[:, None]
    same_owner = (owner[:, :, None] == owner[:, None, :]) & earlier[None, :, :]
    rank = jnp.sum(same_owner.astype(jnp.int32), axis=2)
    target = owner * slots + rank
    slot_columns = jnp.arange(shards * slots, dtype=jnp.int32)
    selected = (target[:, :, None] == slot_columns[None, None, :]) & valid[:, :, None]
    local_ids = history - owner * width
    send_ids = jnp.sum(jnp.where(selected, local_ids[:, :, None], 0), axis=1)
    occupied = jnp.any(selected, axis=1)
    send_ids = jnp.where(occupied, send_ids, width)
    send_weight = jnp.einsum(
        "sp,spj->sj",
        history_weight,
        selected.astype(jnp.bfloat16),
        preferred_element_type=jnp.float32,
    ).astype(jnp.bfloat16)
    got_ids, got_weight = (
        lax.all_to_all(
            send_ids.reshape(seqs, shards, slots), "vocab", split_axis=1, concat_axis=1, tiled=True
        ),
        lax.all_to_all(
            send_weight.reshape(seqs, shards, slots),
            "vocab",
            split_axis=1,
            concat_axis=1,
            tiled=True,
        ),
    )
    got_ids = got_ids.reshape(seqs, shards * slots)
    got_weight = got_weight.reshape(seqs, shards * slots)
    filled = jnp.full((seqs,), shards * slots, jnp.int32)
    counts, weighted = tally(got_ids, got_weight, filled, 0, 0, width)
    seen = counts > 0.5
    scaled = jnp.where(logits > 0, logits / repetition[:, None], logits * repetition[:, None])
    adjusted = (
        jnp.where(seen, scaled, logits)
        - frequency[:, None] * weighted
        - presence[:, None] * seen.astype(jnp.float32)
    )
    local_max = jnp.max(adjusted, axis=1)
    row_max = lax.pmax(local_max, "vocab")
    row_total = lax.psum(jnp.sum(jnp.exp(adjusted - row_max[:, None]), axis=1), "vocab")
    return adjusted - row_max[:, None] - jnp.log(row_total)[:, None]


def solution(mesh):
    return jax.shard_map(
        body,
        mesh=mesh,
        in_specs=(
            P("batch", "vocab"),
            P("batch", "vocab"),
            P("batch", "vocab"),
            P("batch"),
            P("batch"),
            P("batch"),
            P("batch"),
        ),
        out_specs=P("batch", "vocab"),
        check_vma=False,
    )
```

profile of v0, /device:TPU:0, one launch (start us, length us, event | category | flops | bytes accessed | tf_op | source)
XLA Modules:
  0.0 259.8 jit_solution(8279690221531951218)
XLA Ops:
  1.9 18.6 %convert_reduce_fusion = s32[64,512]{1,0:T(8,128)S(1)} fusion(s32[64,512]{1,0:T(8,128)S(1)} %fusion.28, pred[512,512]{1,0:T(8,128)(4,1)S(1)} %iota_compare_fusion.9), kind=kLoop, calls=%fused_computation.36 | loop fusion | flops 67076096 | bytes 524288 | tf_op jit(solution)/shard_map/reduce_sum | solution.py:65
  20.4 1.0 multiply_subtract_fusion
  21.5 38.5 %fusion.21 = bf16[64,1,1024]{2,1,0:T(2,128)(2,1)S(1)} fusion(s32[64,512]{1,0:T(8,128)S(1)} %get-tuple-element.77, pred[64,512]{1,0:T(8,128)(4,1)S(1)} %broadcast_compare_fusion.1, bf16[64,512,1]{1,0,2:T(8,128)(2,1)S(1)} %bitcast.66), kind=kOutput, calls=%fused_computation.33 | convolution fusion | flops 134217728 | bytes 360448 | tf_op jit(solution)/shard_map/sp,spj->sj/dot_general | solution.py:73
  60.6 7.3 %all-to-all-start.1 = ((bf16[64,8,128]{2,0,1:T(8,128)(2,1)}), bf16[64,8,128]{2,0,1:T(8,128)(2,1)S(1)}, u32[]{:S(2)}, u32[]{:S(2)}) async-start(bf16[64,8,128]{2,0,1:T(8,128)(2,1)} %copy_bitcast_fusion.3), calls=%async_computation.1 | async-start | bytes 262144 | tf_op jit(solution)/shard_map/all_to_all | solution.py:83
  68.0 23.5 %fusion.23 = pred[64,1024]{1,0:T(8,128)(4,1)S(1)} fusion(s32[64,512]{1,0:T(8,128)S(1)} %get-tuple-element.77, pred[64,512]{1,0:T(8,128)(4,1)S(1)} %broadcast_compare_fusion.1), kind=kLoop, calls=%fused_computation.34 | loop fusion | flops 100597760 | bytes 229376 | tf_op jit(solution)/shard_map/reduce_or | solution.py:71
  91.5 34.8 %select_reduce_fusion = s32[64,1024]{1,0:T(8,128)S(1)} fusion(s32[64,512]{1,0:T(8,128)S(1)} %get-tuple-element.76, s32[64,512]{1,0:T(8,128)S(1)} %get-tuple-element.77, pred[64,512]{1,0:T(8,128)(4,1)S(1)} %broadcast_compare_fusion.1), kind=kLoop, calls=%fused_computation.30 | loop fusion | flops 134152192 | bytes 557056 | tf_op jit(solution)/shard_map/reduce_sum | solution.py:70
  127.1 6.0 %all-to-all-start = ((s32[64,8,128]{2,0,1:T(8,128)}), s32[64,8,128]{2,0,1:T(8,128)S(1)}, u32[]{:S(2)}, u32[]{:S(2)}) async-start(s32[64,8,128]{2,0,1:T(8,128)} %copy_bitcast_fusion.2), calls=%async_computation | async-start | bytes 524288 | tf_op jit(solution)/shard_map/all_to_all | solution.py:80
  133.2 8.4 %all-to-all-done = s32[64,8,128]{2,0,1:T(8,128)S(1)} async-done(((s32[64,8,128]{2,0,1:T(8,128)}), s32[64,8,128]{2,0,1:T(8,128)S(1)}, u32[]{:S(2)}, u32[]{:S(2)}) %all-to-all-start) | async-done | bytes 262176 | tf_op jit(solution)/shard_map/all_to_all | solution.py:80
  141.8 58.2 %while.12 = (s32[]{:T(128)}, f32[16,4,149,256]{3,2,1,0:T(8,128)}, s32[16,4,1024]{2,1,0:T(4,128)S(1)}, bf16[16,4,1024]{2,1,0:T(4,128)(2,1)S(1)}, s32[]{:T(128)}) while((s32[]{:T(128)}, f32[16,4,149,256]{3,2,1,0:T(8,128)}, s32[16,4,1024]{2,1,0:T(4,128)S(1)}, bf16[16,4,1024]{2,1,0:T(4,128)(2,1)S(1)}, s32[]{:T(128)}) %tuple.33), condition=%wide.region_4.5_spmd, body=%wide.region_3.4_spmd.sunk | while | flops 319512576 | bytes 4964937 | solution.py:40
  142.0 1.4 fusion.49
  144.2 1.3 fusion.51
  145.6 1.4 fusion.49
  147.8 1.3 fusion.51
  149.2 1.4 fusion.49
  151.4 1.4 fusion.51
  152.9 1.4 fusion.49
  155.1 1.3 fusion.51
  156.5 1.4 fusion.49
  158.7 1.3 fusion.51
  160.1 1.4 fusion.49
  162.3 1.3 fusion.51
  163.8 1.4 fusion.49
  166.0 1.3 fusion.51
  167.4 1.4 fusion.49
  169.6 1.3 fusion.51
  171.0 1.4 fusion.49
  173.2 1.3 fusion.51
  174.6 1.4 fusion.49
  176.9 1.3 fusion.51
  178.3 1.4 fusion.49
  180.5 1.3 fusion.51
  181.9 1.4 fusion.49
  184.1 1.3 fusion.51
  185.5 1.4 fusion.49
  187.7 1.3 fusion.51
  189.2 1.4 fusion.49
  191.4 1.4 fusion.51
  192.9 1.4 fusion.49
  195.1 1.4 fusion.51
  196.5 1.4 fusion.49
  198.7 1.3 fusion.51
  200.1 4.6 %fusion.35 = (f32[64,149,128]{2,1,0:T(8,128)S(1)}, f32[64,149,128]{2,1,0:T(8,128)S(1)}) fusion(f32[64,149,256]{2,1,0:T(8,128)} %bitcast.69), kind=kLoop, calls=%fused_computation.63 | loop fusion | bytes 19529728 | tf_op jit(solution)/shard_map/slice | solution.py:49
  204.7 3.9 %copy_bitcast_fusion = (f32[64,19072]{1,0:T(8,128)S(1)}, f32[64,19072]{1,0:T(8,128)}) fusion(f32[8,8,149,128]{3,2,1,0:T(8,128)S(1)} %bitcast.68, f32[8,8,149,128]{3,2,1,0:T(8,128)S(1)} %bitcast.67), kind=kLoop, calls=%fused_computation.38 | loop fusion | bytes 19529728 | tf_op jit(solution)/shard_map/reshape | solution.py:50
  208.6 6.4 %fusion.33 = (f32[64]{0:T(128)S(1)}, f32[64,19008]{1,0:T(8,128)}) fusion(f32[64]{0:T(128)S(1)} %copy-done.1, f32[64,19072]{1,0:T(8,128)S(1)} %get-tuple-element.78, f32[64]{0:T(128)S(1)} %copy-done.2, f32[64,19008]{1,0:T(8,128)} %param.9, f32[64]{0:T(128)S(1)} %copy-done.3, f32[64,19072]{1,0:T(8,128)} %get-tuple-element.79), kind=kLoop, calls=%fused_computation.62 | loop fusion | flops 13381568 | bytes 19465216 | tf_op jit(solution)/shard_map/reduce_max | solution.py:102
  215.0 19.3 %pmax.7 = f32[64]{0:T(128)S(1)} all-reduce(f32[64]{0:T(128)S(1)} %get-tuple-element.72), channel_id=1, replica_groups=mesh['batch'=4,'vocab'=8] {'vocab'}, use_global_device_ids=true, to_apply=%region_6.7 | all-reduce | flops 64 | bytes 512 | tf_op jit(solution)/shard_map/pmax | solution.py:103
  234.3 3.2 %exponential_reduce_fusion = f32[64]{0:T(128)S(1)} fusion(f32[64,19008]{1,0:T(8,128)} %get-tuple-element.73, f32[64]{0:T(128)S(1)} %pmax.7), kind=kLoop, calls=%fused_computation.44 | loop fusion | flops 2432960 | bytes 4866560 | tf_op jit(solution)/shard_map/reduce_sum | solution.py:104
  237.5 17.1 %psum.7 = f32[64]{0:T(128)S(1)} all-reduce(f32[64]{0:T(128)S(1)} %exponential_reduce_fusion), channel_id=1, replica_groups=mesh['batch'=4,'vocab'=8] {'vocab'}, use_global_device_ids=true, to_apply=%region_8.9 | all-reduce | flops 64 | bytes 512 | tf_op jit(solution)/shard_map/psum | solution.py:104
  254.7 5.1 %subtract_subtract_fusion = f32[64,19008]{1,0:T(8,128)} fusion(f32[64,19008]{1,0:T(8,128)} %get-tuple-element.73, f32[64]{0:T(128)S(1)} %log.3, f32[64]{0:T(128)S(1)} %pmax.7), kind=kLoop, calls=%fused_computation.45 | loop fusion | flops 2433024 | bytes 9732608 | tf_op jit(solution)/shard_map/sub | solution.py:105
  (85 shorter events, 17.7 us)
Async XLA Ops:
  0.0 21.5 %copy-start = (bf16[64,512]{1,0:T(8,128)(2,1)S(1)}, bf16[64,512]{1,0:T(8,128)(2,1)}, u32[]{:S(2)}) copy-start(bf16[64,512]{1,0:T(8,128)(2,1)} %param.11) | copy-start | bytes 196612
  60.6 66.4 %all-to-all-start.1 = ((bf16[64,8,128]{2,0,1:T(8,128)(2,1)}), bf16[64,8,128]{2,0,1:T(8,128)(2,1)S(1)}, u32[]{:S(2)}, u32[]{:S(2)}) async-start(bf16[64,8,128]{2,0,1:T(8,128)(2,1)} %copy_bitcast_fusion.3), calls=%async_computation.1 | async-start | bytes 262144 | tf_op jit(solution)/shard_map/all_to_all | solution.py:83
  127.1 14.5 %all-to-all-start = ((s32[64,8,128]{2,0,1:T(8,128)}), s32[64,8,128]{2,0,1:T(8,128)S(1)}, u32[]{:S(2)}, u32[]{:S(2)}) async-start(s32[64,8,128]{2,0,1:T(8,128)} %copy_bitcast_fusion.2), calls=%async_computation | async-start | bytes 524288 | tf_op jit(solution)/shard_map/all_to_all | solution.py:80
  204.6 4.0 %copy-start.1 = (f32[64]{0:T(128)S(1)}, f32[64]{0:T(128)}, u32[]{:S(2)}) copy-start(f32[64]{0:T(128)} %param.15) | copy-start | bytes 772
  204.7 4.0 %copy-start.2 = (f32[64]{0:T(128)S(1)}, f32[64]{0:T(128)}, u32[]{:S(2)}) copy-start(f32[64]{0:T(128)} %param.14) | copy-start | bytes 772
  204.7 4.0 %copy-start.3 = (f32[64]{0:T(128)S(1)}, f32[64]{0:T(128)}, u32[]{:S(2)}) copy-start(f32[64]{0:T(128)} %param.13) | copy-start | bytes 772
where the time goes:
time: 260 us
  other arithmetic  131 us (50%)
  matrix products  59.9 us (23%)
  blocking collectives  36.4 us (14%)
  starting transfers between devices  13.3 us (5%)
  local copies, waits for them, and re-layouts  9.81 us (4%)
  waiting for transfers between devices  8.38 us (3%)
    dot_general x1, matrix products, body(): jnp.einsum('sp,spj->sj', history_weight, selected.astype(jnp.bfloat16), p...  38.5 us
    reduce_sum x1, other arithmetic, body(): send_ids = jnp.sum(jnp.where(selected, local_ids[:, :, None], 0), axis=1)  34.8 us
    reduce_or x1, other arithmetic, body(): occupied = jnp.any(selected, axis=1)  23.5 us
    mul x16, other arithmetic, one_group(): hot_lower * piece_weight[:, :, None]  22.2 us
    dot_general x16, matrix products, one_group(): jnp.einsum('sph,spl->shl', hot_upper, paired, preferred_element_type=jnp....  21.5 us
    pmax x1, blocking collectives, body(): row_max = lax.pmax(local_max, 'vocab')  19.3 us
    reduce_sum x1, other arithmetic, body(): rank = jnp.sum(same_owner.astype(jnp.int32), axis=2)  18.6 us
    psum x1, blocking collectives, body(): lax.psum(jnp.sum(jnp.exp(adjusted - row_max[:, None]), axis=1), 'vocab')  17.1 us
  transfers between devices with their start and end apart: 2, of which 1 were waited for; matrix products, arithmetic and copies ran while one was open for 23% of the time, Pallas kernels for 0%

commit v1 on v0

v1 whole, which is shorter than its diff:
```python
import functools

import jax
import jax.numpy as jnp
from jax import lax
from jax.experimental import pallas as pl
from jax.experimental.pallas import tpu as pltpu
from jax.sharding import PartitionSpec as P

LANES = 128
CHUNK = 256
FIELD = 16
SCALE = 512.0


def column(row, rows):
    wide = jnp.broadcast_to(row, (rows, rows))
    same = lax.broadcasted_iota(jnp.int32, (rows, rows), 0) == lax.broadcasted_iota(
        jnp.int32, (rows, rows), 1
    )
    return jnp.sum(jnp.where(same, wide, 0.0), axis=1, keepdims=True)


def pack_kernel(
    shards, slots, width, ids_hbm, weight_hbm, lengths_hbm, send_ref, ids_ref, weight_ref, lengths_ref, sem
):
    copies = [
        pltpu.make_async_copy(source, target, sem.at[k])
        for k, (source, target) in enumerate(
            ((ids_hbm, ids_ref), (weight_hbm, weight_ref), (lengths_hbm, lengths_ref))
        )
    ]
    for copy in copies:
        copy.start()
    for copy in copies:
        copy.wait()
    rows, span = ids_ref.shape
    tiles = span // LANES
    first = lax.axis_index("vocab") * span
    ids = ids_ref[...]
    lengths = column(lengths_ref[...].astype(jnp.float32), rows)
    positions = (lax.broadcasted_iota(jnp.int32, (rows, span), 1) + first).astype(jnp.float32)
    valid = positions < lengths
    owner = jnp.zeros_like(ids)
    for shard in range(1, shards):
        owner = owner + (ids >= shard * width).astype(jnp.int32)
    code = (weight_ref[...].astype(jnp.float32) * SCALE).astype(jnp.int32)
    payload = ((ids - owner * width) << FIELD) | code
    owner = jnp.where(valid, owner, -1)
    below = lax.broadcasted_iota(jnp.int32, (LANES, LANES), 0) <= lax.broadcasted_iota(
        jnp.int32, (LANES, LANES), 1
    )
    below = below.astype(jnp.float32).astype(jnp.bfloat16)
    lane = lax.broadcasted_iota(jnp.int32, (rows, LANES), 1)
    last = jnp.full((rows, LANES), LANES - 1, jnp.int32)
    for shard in range(shards):
        mine = jnp.concatenate(
            [(owner[:, t * LANES : (t + 1) * LANES] == shard) for t in range(tiles)], axis=0
        )
        mine = jnp.where(mine, 1.0, 0.0).astype(jnp.bfloat16)
        ranks = jnp.dot(mine, below, preferred_element_type=jnp.float32).astype(jnp.int32)
        word = ranks[:rows]
        for t in range(1, tiles):
            word = word | (ranks[t * rows : (t + 1) * rows] << (8 * t))
        totals = jnp.take_along_axis(word, last, axis=1)
        base = jnp.zeros_like(lane)
        shift = jnp.zeros_like(lane)
        start = totals & 255
        for t in range(1, tiles):
            past = lane >= start
            base = jnp.where(past, start, base)
            shift = jnp.where(past, 8 * t, shift)
            start = start + ((totals >> (8 * t)) & 255)
        wanted = lane - base
        place = jnp.zeros_like(lane)
        step = LANES // 2
        while step:
            seen = (jnp.take_along_axis(word, place + (step - 1), axis=1) >> shift) & 255
            place = jnp.where(seen <= wanted, place + step, place)
            step //= 2
        found = jnp.take_along_axis(payload[:, :LANES], place, axis=1)
        for t in range(1, tiles):
            other = jnp.take_along_axis(payload[:, t * LANES : (t + 1) * LANES], place, axis=1)
            found = jnp.where(shift == 8 * t, other, found)
        found = jnp.where(lane < start, found, 0)
        send_ref[shard] = found[:, :slots]


def tally_kernel(
    width, ordered, got_ref, logits_ref, repetition_ref, frequency_ref, presence_ref, adjusted_ref, stats_ref,
    dense, sums, factors, trips, logits_sem, factor_sem,
):
    blocks, rows, _ = got_ref.shape
    groups = rows // 8
    pairs = blocks // 2
    chunks = -(-width // CHUNK)
    uppers = -(-chunks // 16) * 16

    def load(group):
        part = pl.ds(pl.multiple_of(group * 8, 8), 8)
        return pltpu.make_async_copy(logits_ref.at[part], adjusted_ref.at[part], logits_sem.at[group])

    for group in range(groups):
        load(group).start()
    fetches = [
        pltpu.make_async_copy(ref, factors.at[pl.ds(k, 1)], factor_sem.at[k])
        for k, ref in enumerate((repetition_ref, frequency_ref, presence_ref))
    ]
    for fetch in fetches:
        fetch.start()

    lane = lax.broadcasted_iota(jnp.int32, (8, LANES), 1)
    if ordered:
        ones = jnp.ones((LANES, LANES), jnp.bfloat16)

        def merge(group, carry):
            part = pl.ds(pl.multiple_of(group * 8, 8), 8)
            words = [got_ref[block, part, :] for block in range(blocks)]
            full = jnp.concatenate(words, axis=0) > 0
            count = jnp.dot(
                jnp.where(full, 1.0, 0.0).astype(jnp.bfloat16), ones, preferred_element_type=jnp.float32
            ).astype(jnp.int32)
            starts = [jnp.zeros_like(lane)]
            for block in range(blocks):
                starts.append(starts[-1] + count[block * 8 : block * 8 + 8])
            turned = [
                jnp.take_along_axis(words[block], (lane - starts[block]) & (LANES - 1), axis=1)
                for block in range(blocks)
            ]
            for tile in range(blocks):
                spot = lane + tile * LANES
                value = turned[tile]
                for block in range(tile + 1, blocks):
                    value = jnp.where(spot >= starts[block], turned[block], value)
                dense[tile, part, :] = jnp.where(spot < starts[blocks], value, 0)
            most = jnp.max(starts[blocks])
            trips[group] = (most + 2 * LANES - 1) // (2 * LANES)
            return carry

        lax.fori_loop(0, groups, merge, 0)
    else:
        dense[...] = got_ref[...]
        for group in range(groups):
            trips[group] = pairs

    iota = lax.broadcasted_iota(jnp.int32, (CHUNK, LANES), 0).astype(jnp.float32)
    iota = iota.astype(jnp.bfloat16)
    zero = jnp.zeros((), jnp.bfloat16)
    one = jnp.ones((), jnp.bfloat16)

    def spread(array, row, count):
        piece = jnp.broadcast_to(array[row : row + 1], (16, LANES)).astype(jnp.bfloat16)
        return jnp.concatenate([piece] * (count // 16), axis=0)

    def products(group, pair):
        part = pl.ds(pl.multiple_of(group * 8, 8), 8)
        halves = []
        for half in range(2):
            words = dense[pair * 2 + half, part, :]
            local = words >> FIELD
            halves.append((
                (local >> 8).astype(jnp.float32),
                (local & 255).astype(jnp.float32),
                (words & 0xFFFF).astype(jnp.float32) * (1.0 / SCALE),
            ))
        for row in range(8):
            hot_upper, hot_lower = [], []
            for upper_rows, lower_rows, weight_rows in halves:
                upper = spread(upper_rows, row, uppers)
                lower = spread(lower_rows, row, CHUNK)
                weight = spread(weight_rows, row, CHUNK)
                hot_upper.append(jnp.where(upper == iota[:uppers], one, zero))
                hot_lower.append(jnp.where(lower == iota, weight, zero))
            yield row, lax.dot_general(
                jnp.concatenate(hot_upper, axis=1),
                jnp.concatenate(hot_lower, axis=1),
                (((1,), (1,)), ((), ())),
                preferred_element_type=jnp.float32,
            )

    def tally(group, carry):
        for row, total in products(group, 0):
            for half in range(CHUNK // LANES):
                part = total[:, half * LANES : (half + 1) * LANES]
                sums[group, half, pl.ds(row, uppers, stride=8), :] = part

        def more(pair, carry):
            for row, total in products(group, pair):
                for half in range(CHUNK // LANES):
                    part = total[:, half * LANES : (half + 1) * LANES]
                    sums[group, half, pl.ds(row, uppers, stride=8), :] += part
            return carry

        lax.fori_loop(1, trips[group], more, 0)
        return carry

    lax.fori_loop(0, groups, tally, 0)
    for fetch in fetches:
        fetch.wait()

    def penalize(group, spot):
        row0 = pl.multiple_of(group * 8, 8)
        part = pl.ds(row0, 8)
        here = lax.broadcasted_iota(jnp.int32, (8, rows), 1) == row0 + lax.broadcasted_iota(
            jnp.int32, (8, rows), 0
        )

        def mine(k):
            row = jnp.broadcast_to(factors[k : k + 1, :], (8, rows))
            return jnp.sum(jnp.where(here, row, 0.0), axis=1, keepdims=True)

        repetition, frequency, presence = mine(0), mine(1), mine(2)
        inverse = 1.0 / repetition
        best = jnp.full((8, LANES), -jnp.inf, jnp.float32)
        load(group).wait()
        tiles = -(-width // LANES)
        tail = None
        for tile in range(tiles):
            size = min(LANES, width - tile * LANES)
            columns = pl.ds(tile * LANES, size)
            x = adjusted_ref[part, columns]
            chunk, half = divmod(tile, CHUNK // LANES)
            weighted = sums[group, half, chunk * 8 : chunk * 8 + 8, :size]
            scaled = x * jnp.where(x > 0, inverse, repetition)
            value = jnp.where(weighted > 0, scaled - presence, x) - frequency * weighted
            adjusted_ref[part, columns] = value
            if size == LANES:
                best = jnp.maximum(best, value)
            else:
                tail = jnp.max(value, axis=1, keepdims=True)
        top = jnp.max(best, axis=1, keepdims=True)
        if tail is not None:
            top = jnp.maximum(top, tail)
        total = jnp.zeros((8, LANES), jnp.float32)
        rest = jnp.zeros((8, 1), jnp.float32)
        for tile in range(tiles):
            size = min(LANES, width - tile * LANES)
            value = jnp.exp(adjusted_ref[part, pl.ds(tile * LANES, size)] - top)
            if size == LANES:
                total = total + value
            else:
                rest = jnp.sum(value, axis=1, keepdims=True)
        rest = rest + jnp.sum(total, axis=1, keepdims=True)
        line = lax.broadcasted_iota(jnp.int32, (8, 2 * rows), 1)
        seq = row0 + lax.broadcasted_iota(jnp.int32, (8, 2 * rows), 0)
        return spot + jnp.where(line == seq, top, 0.0) + jnp.where(line == seq + rows, rest, 0.0)

    spot = lax.fori_loop(0, groups, penalize, jnp.zeros((8, 2 * rows), jnp.float32))
    spot = jnp.sum(spot, axis=0, keepdims=True)
    stats_ref[...] = jnp.broadcast_to(spot, stats_ref.shape)


def finish_kernel(adjusted_ref, stats_ref, out_ref, result, sem):
    rows = adjusted_ref.shape[0]
    tops = stats_ref[:, :rows]
    totals = stats_ref[:, rows:]
    top = jnp.max(tops, axis=0, keepdims=True)
    total = jnp.log(jnp.sum(totals * jnp.exp(tops - top), axis=0, keepdims=True))
    top, total = column(top, rows), column(total, rows)
    copies = []
    for group in range(rows // 8):
        part = slice(group * 8, group * 8 + 8)
        result[part, :] = adjusted_ref[part, :] - top[part] - total[part]
        copies.append(pltpu.make_async_copy(result.at[part], out_ref.at[part], sem.at[group]))
        copies[-1].start()
    for copy in copies:
        copy.wait()


def vmem(shape, dtype):
    return pltpu.VMEM(shape, dtype)


def outside(array):
    return pltpu.with_memory_space_constraint(array, pltpu.HBM)


def body(logits, history, history_weight, lengths, repetition, frequency, presence):
    rows, width = logits.shape
    span = history.shape[1]
    shards = lax.axis_size("vocab")
    slots = max(2, 2 * span // shards)
    full = pl.BlockSpec(memory_space=pltpu.VMEM)
    away = pl.BlockSpec(memory_space=pltpu.HBM)
    ordered = slots % LANES == 0
    send = pl.pallas_call(
        functools.partial(pack_kernel, shards, slots, width),
        out_shape=vmem((shards, rows, slots), jnp.int32),
        in_specs=[away] * 3,
        out_specs=full,
        scratch_shapes=[
            vmem((rows, span), jnp.int32),
            vmem((rows, span), jnp.bfloat16),
            vmem((1, rows), jnp.int32),
            pltpu.SemaphoreType.DMA((3,)),
        ],
        compiler_params=pltpu.CompilerParams(vmem_limit_bytes=8 << 20),
        name="pack",
    )(outside(history), outside(history_weight), outside(lengths.reshape(1, rows)))
    got = lax.all_to_all(send, "vocab", split_axis=0, concat_axis=0, tiled=True)
    if ordered:
        got = got.reshape(shards, rows, slots // LANES, LANES).transpose(0, 2, 1, 3)
        got = got.reshape(-1, rows, LANES)
    else:
        got = got.transpose(1, 0, 2).reshape(rows, shards * slots)
        got = jnp.pad(got, ((0, 0), (0, -(shards * slots) % LANES)))
        got = got.reshape(rows, -1, LANES).transpose(1, 0, 2)
    if got.shape[0] % 2:
        got = jnp.pad(got, ((0, 1), (0, 0), (0, 0)))
    groups = rows // 8
    uppers = -(-(-(-width // CHUNK)) // 16) * 16
    adjusted, stats = pl.pallas_call(
        functools.partial(tally_kernel, width, ordered),
        out_shape=(vmem((rows, width), jnp.float32), vmem((shards, 2 * rows), jnp.float32)),
        in_specs=[full] + [away] * 4,
        out_specs=(full, full),
        scratch_shapes=[
            vmem(got.shape, jnp.int32),
            vmem((groups, CHUNK // LANES, uppers * 8, LANES), jnp.float32),
            vmem((3, rows), jnp.float32),
            pltpu.SMEM((groups,), jnp.int32),
            pltpu.SemaphoreType.DMA((groups,)),
            pltpu.SemaphoreType.DMA((3,)),
        ],
        compiler_params=pltpu.CompilerParams(vmem_limit_bytes=24 << 20),
        name="tally",
    )(
        got,
        outside(logits),
        outside(repetition.reshape(1, rows)),
        outside(frequency.reshape(1, rows)),
        outside(presence.reshape(1, rows)),
    )
    stats = lax.all_to_all(stats, "vocab", split_axis=0, concat_axis=0, tiled=True)
    return pl.pallas_call(
        finish_kernel,
        out_shape=jax.ShapeDtypeStruct((rows, width), jnp.float32),
        in_specs=[full, full],
        out_specs=away,
        scratch_shapes=[vmem((rows, width), jnp.float32), pltpu.SemaphoreType.DMA((groups,))],
        compiler_params=pltpu.CompilerParams(vmem_limit_bytes=24 << 20),
        name="finish",
    )(adjusted, stats)


def solution(mesh):
    return jax.shard_map(
        body,
        mesh=mesh,
        in_specs=(
            P("batch", "vocab"),
            P("batch", "vocab"),
            P("batch", "vocab"),
            P("batch"),
            P("batch"),
            P("batch"),
            P("batch"),
        ),
        out_specs=P("batch", "vocab"),
        check_vma=False,
    )
```

time: 260 us -> 48.7 us (0.19)
  other arithmetic: 131 us -> 0 us
  matrix products: 59.9 us -> 0 us
  Pallas kernels: 0 us -> 23.3 us
  starting transfers between devices: 13.3 us -> 0 us
  blocking collectives: 36.4 us -> 24.9 us
  local copies, waits for them, and re-layouts: 9.81 us -> 0 us
  waiting for transfers between devices: 8.38 us -> 0 us
    dot_general x17 -> x0, matrix products: 59.9 us -> none  [the longest x1 38.5 us: body(): jnp.einsum('sp,spj->sj', history_weight, selected.astype(jnp.bfloat16), p...]
    reduce_sum x3 -> x0, other arithmetic: 56.6 us -> none  [the longest x1 34.8 us: body(): send_ids = jnp.sum(jnp.where(selected, local_ids[:, :, None], 0), axis=1)]
    all_to_all x0 -> x2, blocking collectives: none -> 24.9 us  [the longest x1 16 us: body(): got = lax.all_to_all(send, 'vocab', split_axis=0, concat_axis=0, tiled=True)]
    reduce_or x1 -> x0, other arithmetic: 23.5 us -> none  [body(): occupied = jnp.any(selected, axis=1)]
    pallas_call x0 -> x3, Pallas kernels: none -> 23.3 us  [the longest x1 17.2 us: body(): pl.pallas_call(functools.partial(tally_kernel, width, ordered), out_shape...]
    mul x16 -> x0, other arithmetic: 22.2 us -> none  [one_group(): hot_lower * piece_weight[:, :, None]]
    pmax x1 -> x0, blocking collectives: 19.3 us -> none  [body(): row_max = lax.pmax(local_max, 'vocab')]
    psum x1 -> x0, blocking collectives: 17.1 us -> none  [body(): lax.psum(jnp.sum(jnp.exp(adjusted - row_max[:, None]), axis=1), 'vocab')]
  transfers between devices with their start and end apart: 2 -> 0, of which waited for: 1 -> 0; matrix products, arithmetic and copies ran while one was open for 23% -> 0% of each run, Pallas kernels for 0% -> 0%
where the time goes in v1:
time: 48.7 us; the launch traced here: 48.2 us
  blocking collectives  24.9 us (51%)
  Pallas kernels  23.3 us (48%)
    pallas_call x1, Pallas kernels, body(): pl.pallas_call(functools.partial(tally_kernel, width, ordered), out_shape...  17.2 us
    all_to_all x1, blocking collectives, body(): got = lax.all_to_all(send, 'vocab', split_axis=0, concat_axis=0, tiled=True)  16 us
    all_to_all x1, blocking collectives, body(): lax.all_to_all(stats, 'vocab', split_axis=0, concat_axis=0, tiled=True)  8.9 us
    pallas_call x1, Pallas kernels, body(): pl.pallas_call(functools.partial(pack_kernel, shards, slots, width), out_...  3.53 us
    pallas_call x1, Pallas kernels, body(): pl.pallas_call(finish_kernel, out_shape=jax.ShapeDtypeStruct((rows, width...  2.58 us

profile of v1, /device:TPU:0, one launch (start us, length us, event | category | flops | bytes accessed | tf_op | source)
XLA Modules:
  0.0 48.2 jit_solution(12178552943600228226)
XLA Ops:
  0.0 3.5 %pack.1 = s32[8,64,128]{2,1,0:T(8,128)S(1)} custom-call(s32[64,512]{1,0:T(8,128)} %ids_hbm.1, bf16[64,512]{1,0:T(8,128)(2,1)} %weight_hbm.1, s32[1,64]{1,0:T(1,128)} %bitcast.13), custom_call_target="tpu_custom_call" | custom-call | tf_op jit(solution)/shard_map/pack/pallas_call | solution.py:286
  3.5 16.0 %all_to_all.16.got_ref = s32[8,64,128]{2,1,0:T(8,128)S(1)} all-to-all(s32[8,64,128]{2,1,0:T(8,128)S(1)} %pack.1), channel_id=1, replica_groups=mesh['batch'=4,'vocab'=8] {'vocab'}, dimensions={0} | all-to-all | bytes 524288 | tf_op jit(solution)/shard_map/all_to_all | solution.py:300
  19.6 17.2 %tally.1 = (f32[64,19008]{1,0:T(8,128)S(1)}, f32[8,128]{1,0:T(8,128)S(1)}) custom-call(s32[8,64,128]{2,1,0:T(8,128)S(1)} %all_to_all.16.got_ref, f32[64,19008]{1,0:T(8,128)} %logits_ref.1, f32[1,64]{1,0:T(1,128)} %bitcast.10, f32[1,64]{1,0:T(1,128)} %bitcast.11, f32[1,64]{1,0:T(1,128)} %bitcast.12), custom_call_target="tpu_custom_call" | custom-call | tf_op jit(solution)/shard_map/tally/pallas_call | solution.py:312
  36.8 8.9 %all_to_all.17 = f32[8,1,128]{2,1,0:T(1,128)S(1)} all-to-all(f32[8,1,128]{2,1,0:T(1,128)S(1)} %bitcast.9), channel_id=1, replica_groups=mesh['batch'=4,'vocab'=8] {'vocab'}, dimensions={0} | all-to-all | bytes 8192 | tf_op jit(solution)/shard_map/all_to_all | solution.py:334
  45.7 2.6 %finish.1 = f32[64,19008]{1,0:T(8,128)} custom-call(f32[64,19008]{1,0:T(8,128)S(1)} %get-tuple-element.7.adjusted_ref, f32[8,128]{1,0:T(8,128)S(1)} %bitcast.8), custom_call_target="tpu_custom_call" | custom-call | tf_op jit(solution)/shard_map/finish/pallas_call | solution.py:335
